TPU v7x, 32 devices: a whole 2x2x4 slice. The times are simulated.
32 devices in a mesh: group: 2 (over y), seq: 4 (over z), dp: 2 (over x), head: 2 (over core).
Axes of the slice: x: 2, y: 2, z: 4, core: 2. Of those that a mesh axis runs over, the one named last changes fastest.
Arguments:
- query_raw: bfloat16 [4, 512, 2048], P(('group', 'dp'), 'seq', 'head'), parts along dimension 0, may hold values from -6 to 6
- key_raw: bfloat16 [4, 512, 2048], P(('group', 'dp'), 'seq', 'head'), parts along dimension 0, may hold values from -6 to 6
- value_raw: bfloat16 [4, 512, 2048], P(('group', 'dp'), 'seq', 'head'), parts along dimension 0, may hold values from -12 to 12
- conv_weight: float32 [3, 4, 2048], P(None, None, 'head'), may hold values from -2.4 to 2.4
- beta_logit: float32 [4, 16, 512], P(('group', 'dp'), 'head', 'seq'), parts along dimension 0, may hold values from -14 to 9
- cotangent: bfloat16 [4, 512, 2048], P(('group', 'dp'), 'seq', 'head'), parts along dimension 0, may hold values from -6 to 6
Outputs:
- mixed: float32 [4, 512, 2048], P(('group', 'dp'), 'seq', 'head'), parts along dimension 0
- query_grad: bfloat16 [4, 512, 2048], P(('group', 'dp'), 'seq', 'head'), parts along dimension 0
- key_grad: bfloat16 [4, 512, 2048], P(('group', 'dp'), 'seq', 'head'), parts along dimension 0
- value_grad: bfloat16 [4, 512, 2048], P(('group', 'dp'), 'seq', 'head'), parts along dimension 0
- beta_grad: float32 [4, 16, 512], P(('group', 'dp'), 'head', 'seq'), parts along dimension 0
- conv_grad: float32 [6, 4, 16, 128], P('group', None, 'head', ('seq', 'dp')), parts along dimension 0
There are 2 independent parts, one for each index of `group`. A program takes and returns all parts, laid end to end along the dimension named above; an argument that names none is the same for every part. Nothing has to cross between parts.
All inputs are finite; a program needn't handle non-finite values.
Results may differ from a plain program's by a relative error of at most 0.0023.
Values may be sent and summed in bfloat16 or wider, within the bound.
A program may use at most 128 MiB of HBM per device.

v0:
```python
import jax
import jax.numpy as jnp
from jax import lax
from jax.sharding import PartitionSpec as P

SPAN = 64


def from_behind(array, axis, by):
    length = lax.axis_size(axis)
    pairs = [(i, i + by) for i in range(length) if 0 <= i + by < length]
    return lax.ppermute(array, axis, pairs)


def strict_lower(count):
    return jnp.tril(jnp.ones((count, count), jnp.float32), -1)


def solve_block(lookup_vectors, payload_vectors, betas):
    count = lookup_vectors.shape[-2]
    width = lookup_vectors.shape[-1]
    inner = jnp.einsum(
        "...id,...jd->...ij", lookup_vectors, lookup_vectors, precision=lax.Precision.HIGHEST
    )
    lower_part = betas[..., :, None] * inner * strict_lower(count)
    eye_block = jnp.eye(count, dtype=jnp.float32)
    inverse = eye_block - lower_part
    power_term = lower_part
    reach = 2
    while reach < count:
        power_term = jnp.einsum(
            "...ij,...jk->...ik", power_term, power_term, precision=lax.Precision.HIGHEST
        )
        inverse = jnp.einsum(
            "...ij,...jk->...ik", inverse, eye_block + power_term, precision=lax.Precision.HIGHEST
        )
        reach = reach * 2
    right_side = betas[..., :, None] * jnp.concatenate([lookup_vectors, payload_vectors], axis=-1)
    solved = jnp.einsum("...ij,...jk->...ik", inverse, right_side, precision=lax.Precision.HIGHEST)
    return (solved[..., :width], solved[..., width:])


def block_step(memory, inputs):
    queries, lookup_vectors, payload_vectors, betas = inputs
    w_rows, u_rows = solve_block(lookup_vectors, payload_vectors, betas)
    corrected = u_rows - jnp.einsum(
        "...cd,...de->...ce", w_rows, memory, precision=lax.Precision.HIGHEST
    )
    count = lookup_vectors.shape[-2]
    causal = jnp.tril(jnp.ones((count, count), jnp.float32))
    scores = (
        jnp.einsum("...id,...jd->...ij", queries, lookup_vectors, precision=lax.Precision.HIGHEST)
        * causal
    )
    result = jnp.einsum("...cd,...de->...ce", queries, memory, precision=lax.Precision.HIGHEST)
    result = result + jnp.einsum(
        "...ij,...je->...ie", scores, corrected, precision=lax.Precision.HIGHEST
    )
    memory = memory + jnp.einsum(
        "...cd,...ce->...de", lookup_vectors, corrected, precision=lax.Precision.HIGHEST
    )
    return (memory, result)


def absorb(carry, inputs):
    transition, written = carry
    lookup_vectors, payload_vectors, betas = inputs
    w_rows, u_rows = solve_block(lookup_vectors, payload_vectors, betas)
    removal = jnp.einsum(
        "...cd,...ce->...de", lookup_vectors, w_rows, precision=lax.Precision.HIGHEST
    )
    transition = transition - jnp.einsum(
        "...ij,...jk->...ik", removal, transition, precision=lax.Precision.HIGHEST
    )
    written = written - jnp.einsum(
        "...ij,...jk->...ik", removal, written, precision=lax.Precision.HIGHEST
    )
    written = written + jnp.einsum(
        "...cd,...ce->...de", lookup_vectors, u_rows, precision=lax.Precision.HIGHEST
    )
    return ((transition, written), w_rows)


def pull_adjoint(adjoint, inputs):
    queries, lookup_vectors, w_rows, cot = inputs
    count = lookup_vectors.shape[-2]
    causal = jnp.tril(jnp.ones((count, count), jnp.float32))
    scores = (
        jnp.einsum("...id,...jd->...ij", queries, lookup_vectors, precision=lax.Precision.HIGHEST)
        * causal
    )
    reader = queries - jnp.einsum(
        "...ij,...jd->...id", scores, w_rows, precision=lax.Precision.HIGHEST
    )
    keyed = jnp.einsum(
        "...cd,...de->...ce", lookup_vectors, adjoint, precision=lax.Precision.HIGHEST
    )
    adjoint = adjoint - jnp.einsum(
        "...cd,...ce->...de", w_rows, keyed, precision=lax.Precision.HIGHEST
    )
    adjoint = adjoint + jnp.einsum(
        "...cd,...ce->...de", reader, cot, precision=lax.Precision.HIGHEST
    )
    return (adjoint, None)


def to_blocks(active, heads):
    batch, length, total = active.shape
    width = total // heads
    return active.reshape(batch, length // SPAN, SPAN, heads, width).transpose(1, 0, 3, 2, 4)


def from_blocks(blocks):
    count, batch, heads, block_len, width = blocks.shape
    return blocks.transpose(1, 0, 3, 2, 4).reshape(batch, count * block_len, heads * width)


def normalize(blocks):
    return blocks * lax.rsqrt(jnp.sum(blocks * blocks, axis=-1, keepdims=True) + 1e-06)


def prepare(query_ext, key_ext, value_ext, taps_all, logits):
    heads = logits.shape[1]
    margin = taps_all.shape[1] - 1
    length = query_ext.shape[1] - margin

    def convolve(series, taps):
        total = taps[0][None, None, :] * series[:, 0:length]
        for offset in range(1, margin + 1):
            total = total + taps[offset][None, None, :] * series[:, offset : offset + length]
        return total

    queries = normalize(to_blocks(jax.nn.silu(convolve(query_ext, taps_all[0])), heads))
    lookup_vectors = normalize(to_blocks(jax.nn.silu(convolve(key_ext, taps_all[1])), heads))
    payload_vectors = to_blocks(jax.nn.silu(convolve(value_ext, taps_all[2])), heads)
    batch = logits.shape[0]
    betas = jax.nn.sigmoid(logits).reshape(batch, heads, length // SPAN, SPAN).transpose(2, 0, 1, 3)
    return (queries, lookup_vectors, payload_vectors, betas)


def local_pass(query_ext, key_ext, value_ext, taps_all, logits, start):
    blocks = prepare(query_ext, key_ext, value_ext, taps_all, logits)
    final, outputs = lax.scan(block_step, start, blocks)
    return (from_blocks(outputs), final)


def per_device(query_raw, key_raw, value_raw, conv_weight, beta_logit, cotangent):
    heads = beta_logit.shape[1]
    width = query_raw.shape[2] // heads
    batch = query_raw.shape[0]
    margin = conv_weight.shape[1] - 1
    tails = from_behind(
        (query_raw[:, -margin:], key_raw[:, -margin:], value_raw[:, -margin:]), "seq", 1
    )
    query_ext = jnp.concatenate([tails[0], query_raw], axis=1).astype(jnp.float32)
    key_ext = jnp.concatenate([tails[1], key_raw], axis=1).astype(jnp.float32)
    value_ext = jnp.concatenate([tails[2], value_raw], axis=1).astype(jnp.float32)
    cot_full = cotangent.astype(jnp.float32)
    cot_blocks = to_blocks(cot_full, heads)
    queries, lookup_vectors, payload_vectors, betas = prepare(
        query_ext, key_ext, value_ext, conv_weight, beta_logit
    )
    zero_state = jnp.zeros((batch, heads, width, width), jnp.float32)
    identity = jnp.broadcast_to(jnp.eye(width, dtype=jnp.float32), zero_state.shape)
    (transition, written), w_blocks = lax.scan(
        absorb, (identity, zero_state), (lookup_vectors, payload_vectors, betas)
    )
    source = lax.scan(
        pull_adjoint, zero_state, (queries, lookup_vectors, w_blocks, cot_blocks), reverse=True
    )[0]
    shards = lax.axis_size("seq")

    def forward_hop(step, state_in):
        state_out = (
            jnp.einsum("...ij,...jk->...ik", transition, state_in, precision=lax.Precision.HIGHEST)
            + written
        )
        return from_behind(state_out, "seq", 1)

    def backward_hop(step, adjoint_out):
        adjoint_in = (
            jnp.einsum(
                "...ji,...jk->...ik", transition, adjoint_out, precision=lax.Precision.HIGHEST
            )
            + source
        )
        return from_behind(adjoint_in, "seq", -1)

    incoming = lax.fori_loop(0, shards - 1, forward_hop, zero_state)
    outgoing = lax.fori_loop(0, shards - 1, backward_hop, zero_state)
    (mixed, final), pullback = jax.vjp(
        local_pass, query_ext, key_ext, value_ext, conv_weight, beta_logit, incoming
    )
    grads = pullback((cot_full, outgoing))
    returned = (
        from_behind(grads[0][:, :margin].astype(jnp.bfloat16), "seq", -1).astype(jnp.float32),
        from_behind(grads[1][:, :margin].astype(jnp.bfloat16), "seq", -1).astype(jnp.float32),
        from_behind(grads[2][:, :margin].astype(jnp.bfloat16), "seq", -1).astype(jnp.float32),
    )

    def finish(grad_ext, extra):
        return grad_ext[:, margin:].at[:, -margin:].add(extra).astype(jnp.bfloat16)

    conv_terms = grads[3].reshape(3, conv_weight.shape[1], heads, width)
    conv_grad = lax.psum_scatter(conv_terms, ("seq", "dp"), scatter_dimension=3, tiled=True)
    return (
        mixed,
        finish(grads[0], returned[0]),
        finish(grads[1], returned[1]),
        finish(grads[2], returned[2]),
        grads[4],
        conv_grad,
    )


def solution(mesh):
    in_specs = (
        P(("group", "dp"), "seq", "head"),
        P(("group", "dp"), "seq", "head"),
        P(("group", "dp"), "seq", "head"),
        P(None, None, "head"),
        P(("group", "dp"), "head", "seq"),
        P(("group", "dp"), "seq", "head"),
    )
    out_specs = (
        P(("group", "dp"), "seq", "head"),
        P(("group", "dp"), "seq", "head"),
        P(("group", "dp"), "seq", "head"),
        P(("group", "dp"), "seq", "head"),
        P(("group", "dp"), "head", "seq"),
        P("group", None, "head", ("seq", "dp")),
    )
    return jax.shard_map(
        per_device, mesh=mesh, in_specs=in_specs, out_specs=out_specs, check_vma=False
    )
```

profile of v0, /device:TPU:0, one launch (start us, length us, event | category | flops | bytes accessed | tf_op | source)
XLA Modules:
  0.0 367.0 jit_solution(12657498974524608596)
XLA Ops:
  7.9 5.1 %collective-permute-start.4 = (bf16[1,3,1024]{2,1,0:T(4,128)(2,1)S(1)}, bf16[1,3,1024]{2,1,0:T(4,128)(2,1)S(1)}, u32[]{:S(2)}, u32[]{:S(2)}) collective-permute-start(bf16[1,3,1024]{2,1,0:T(4,128)(2,1)S(1)} %slice.266), channel_id=1, source_target_pairs={{0,4},{4,8},{8,12},{1,5},{5,9},{9,13},{2,6},{6,10},{10,14},{3,7},{... | collective-permute-start | bytes 18440 | tf_op jit(solution)/shard_map/ppermute | solution.py:12
  13.7 3.5 collective-permute-start.2
  17.9 3.5 collective-permute-start.3
  32.1 27.1 %while.146 = (s32[]{:T(128)}, f32[1,8,128,128]{3,2,1,0:T(8,128)S(1)}, f32[1,8,128,128]{3,2,1,0:T(8,128)}, f32[2,1,8,64,128]{4,3,2,1,0:T(8,128)}, f32[2,1,8,64,12...) while((s32[]{:T(128)}, ...), condition=%wide.region_2.3_spmd.clone, body=%wide.region_1.2_spmd.clone.sunk | while | flops 1007829056 | bytes 21767392 | solution.py:165
  60.0 11.0 %while.147 = (s32[]{:T(128)}, f32[1,8,128,128]{3,2,1,0:T(8,128)S(1)}, f32[2,1,8,64,128]{4,3,2,1,0:T(8,128)}, f32[2,1,8,64,128]{4,3,2,1,0:T(8,128)S(1)}, f32[2,1,...) while((s32[]{:T(128)}, ...), condition=%wide.region_9.10_spmd.clone, body=%wide.region_8.9_spmd.clone.sunk | while | flops 403283968 | bytes 5818488 | solution.py:168
  72.1 49.8 %while.143 = (s32[]{:T(128)}, f32[1,8,128,128]{3,2,1,0:T(8,128)S(1)}, f32[1,8,128,128]{2,3,1,0:T(8,128)}, f32[1,8,128,128]{3,2,1,0:T(8,128)S(1)}, s32[]{:T(128)}) while((s32[]{:T(128)}, f32[1,8,128,128]{3,2,1,0:T(8,128)S(1)}, f32[1,8,128,128]{2,3,1,0:T(8,128)}, f32[1,8,128,128]{3,2,1,0:T(8,128)S(1)}, s32[]{:T(128)}) %tuple.274), condition=%wide.region_11.12_spmd, body=%wide.region_10.11_spmd.sunk | while | flops 201457664 | bytes 4194405 | solution.py:190
  72.5 2.5 fusion.559
  76.3 13.6 %collective-permute-done.1 = f32[1,8,128,128]{3,2,1,0:T(8,128)S(1)} collective-permute-done((f32[1,8,128,128]{3,2,1,0:T(8,128)}, f32[1,8,128,128]{3,2,1,0:T(8,128)S(1)}, u32[]{:S(2)}, u32[]{:S(2)}) %collective-permute-start.1) | collective-permute-done | bytes 524320 | tf_op jit(solution)/shard_map/while/body/eval_jaxpr/ppermute | solution.py:12
  89.9 2.5 fusion.559
  93.7 12.7 %collective-permute-done.1 = f32[1,8,128,128]{3,2,1,0:T(8,128)S(1)} collective-permute-done((f32[1,8,128,128]{3,2,1,0:T(8,128)}, f32[1,8,128,128]{3,2,1,0:T(8,128)S(1)}, u32[]{:S(2)}, u32[]{:S(2)}) %collective-permute-start.1) | collective-permute-done | bytes 524320 | tf_op jit(solution)/shard_map/while/body/eval_jaxpr/ppermute | solution.py:12
  110.2 11.8 %collective-permute-done.1 = f32[1,8,128,128]{3,2,1,0:T(8,128)S(1)} collective-permute-done((f32[1,8,128,128]{3,2,1,0:T(8,128)}, f32[1,8,128,128]{3,2,1,0:T(8,128)S(1)}, u32[]{:S(2)}, u32[]{:S(2)}) %collective-permute-start.1) | collective-permute-done | bytes 524320 | tf_op jit(solution)/shard_map/while/body/eval_jaxpr/ppermute | solution.py:12
  122.2 41.2 %while.142 = (s32[]{:T(128)}, f32[1,8,128,128]{3,2,1,0:T(8,128)S(1)}, f32[1,8,128,128]{3,2,1,0:T(8,128)S(1)}, f32[1,8,128,128]{3,2,1,0:T(8,128)}, s32[]{:T(128)}) while((s32[]{:T(128)}, f32[1,8,128,128]{3,2,1,0:T(8,128)S(1)}, f32[1,8,128,128]{3,2,1,0:T(8,128)S(1)}, f32[1,8,128,128]{3,2,1,0:T(8,128)}, s32[]{:T(128)}) %tuple.265), condition=%wide.region_4.5_spmd, body=%wide.region_3.4_spmd.sunk | while | flops 201457664 | bytes 4194405 | solution.py:189
  122.2 2.5 fusion.556
  124.7 2.8 collective-permute-start
  127.5 8.1 %collective-permute-done = f32[1,8,128,128]{3,2,1,0:T(8,128)S(1)} collective-permute-done((f32[1,8,128,128]{3,2,1,0:T(8,128)}, f32[1,8,128,128]{3,2,1,0:T(8,128)S(1)}, u32[]{:S(2)}, u32[]{:S(2)}) %collective-permute-start) | collective-permute-done | bytes 524320 | tf_op jit(solution)/shard_map/while/body/eval_jaxpr/ppermute | solution.py:12
  135.6 2.5 fusion.556
  138.1 4.3 %collective-permute-start = (f32[1,8,128,128]{3,2,1,0:T(8,128)}, f32[1,8,128,128]{3,2,1,0:T(8,128)S(1)}, u32[]{:S(2)}, u32[]{:S(2)}) collective-permute-start(f32[1,8,128,128]{3,2,1,0:T(8,128)} %fusion.556), channel_id=1, source_target_pairs={{0,4},{4,8},{8,12},{1,5},{5,9},{9,13},{2,6},{6,10},{10,14},{3,7},{... | collective-permute-start | bytes 1572872 | tf_op jit(solution)/shard_map/while/body/eval_jaxpr/ppermute | solution.py:12
  142.4 7.2 %collective-permute-done = f32[1,8,128,128]{3,2,1,0:T(8,128)S(1)} collective-permute-done((f32[1,8,128,128]{3,2,1,0:T(8,128)}, f32[1,8,128,128]{3,2,1,0:T(8,128)S(1)}, u32[]{:S(2)}, u32[]{:S(2)}) %collective-permute-start) | collective-permute-done | bytes 524320 | tf_op jit(solution)/shard_map/while/body/eval_jaxpr/ppermute | solution.py:12
  149.6 2.5 fusion.556
  152.1 4.3 %collective-permute-start = (f32[1,8,128,128]{3,2,1,0:T(8,128)}, f32[1,8,128,128]{3,2,1,0:T(8,128)S(1)}, u32[]{:S(2)}, u32[]{:S(2)}) collective-permute-start(f32[1,8,128,128]{3,2,1,0:T(8,128)} %fusion.556), channel_id=1, source_target_pairs={{0,4},{4,8},{8,12},{1,5},{5,9},{9,13},{2,6},{6,10},{10,14},{3,7},{... | collective-permute-start | bytes 1572872 | tf_op jit(solution)/shard_map/while/body/eval_jaxpr/ppermute | solution.py:12
  156.4 7.0 %collective-permute-done = f32[1,8,128,128]{3,2,1,0:T(8,128)S(1)} collective-permute-done((f32[1,8,128,128]{3,2,1,0:T(8,128)}, f32[1,8,128,128]{3,2,1,0:T(8,128)S(1)}, u32[]{:S(2)}, u32[]{:S(2)}) %collective-permute-start) | collective-permute-done | bytes 524320 | tf_op jit(solution)/shard_map/while/body/eval_jaxpr/ppermute | solution.py:12
  166.0 48.6 %while.145 = (s32[]{:T(128)}, f32[1,8,128,128]{3,2,1,0:T(8,128)S(1)}, f32[2,1,8,64,128]{4,3,2,1,0:T(8,128)}, f32[2,1,8,64,64]{4,3,2,1,0:T(8,128)}, f32[2,1,8,64,...) while((s32[]{:T(128)}, ...), condition=%wide.region_7.8_spmd.clone.clone, body=%wide.region_6.7_spmd.clone.clone.sunk | while | flops 806838272 | bytes 96748824 | solution.py:143
  217.2 65.3 %while.144 = (s32[]{:T(128)}, f32[1,8,128,128]{2,3,1,0:T(8,128)S(1)}, f32[2,1,8,64,128]{4,3,2,1,0:T(8,128)}, f32[2,1,8,64,128]{4,3,2,1,0:T(8,128)}, f32[2,1,8,64...) while((s32[]{:T(128)}, ...), condition=%wide.region_15.16_spmd.clone, body=%wide.region_12.15_spmd.clone.sunk | while | flops 1612627456 | bytes 80601520 | solution.py:143
  310.8 47.6 %reduce-scatter.4.cloned.1.call-done = f32[16,96]{1,0:T(8,128)} async-done(((f32[128,96]{1,0:T(8,128)}), f32[16,96]{1,0:T(8,128)}) %reduce-scatter.4.cloned.1.call-update) | async-done | bytes 6160
  (680 shorter events, 204.6 us)
Async XLA Ops:
  7.2 351.2 %reduce-scatter.4.cloned.1.call-start = ((), (), s32[]{:S(2)}) async-start(), calls=%async_computation.1 | async-start | bytes 73728
  7.9 13.5 %copy-start.100 = (f32[3,4,1024]{2,1,0:T(4,128)S(1)}, f32[3,4,1024]{2,1,0:T(4,128)}, u32[]{:S(2)}) copy-start(f32[3,4,1024]{2,1,0:T(4,128)} %param.27) | copy-start | bytes 147460
  7.9 15.8 %collective-permute-start.4 = (bf16[1,3,1024]{2,1,0:T(4,128)(2,1)S(1)}, bf16[1,3,1024]{2,1,0:T(4,128)(2,1)S(1)}, u32[]{:S(2)}, u32[]{:S(2)}) collective-permute-start(bf16[1,3,1024]{2,1,0:T(4,128)(2,1)S(1)} %slice.266), channel_id=1, source_target_pairs={{0,4},{4,8},{8,12},{1,5},{5,9},{9,13},{2,6},{6,10},{10,14},{3,7},{... | collective-permute-start | bytes 18440 | tf_op jit(solution)/shard_map/ppermute | solution.py:12
  13.7 12.3 %collective-permute-start.2 = (bf16[1,3,1024]{2,1,0:T(4,128)(2,1)S(1)}, bf16[1,3,1024]{2,1,0:T(4,128)(2,1)S(1)}, u32[]{:S(2)}, u32[]{:S(2)}) collective-permute-start(bf16[1,3,1024]{2,1,0:T(4,128)(2,1)S(1)} %slice.248), channel_id=1, source_target_pairs={{0,4},{4,8},{8,12},{1,5},{5,9},{9,13},{2,6},{6,10},{10,14},{3,7},{... | collective-permute-start | bytes 18440 | tf_op jit(solution)/shard_map/ppermute | solution.py:12
  17.9 10.6 %collective-permute-start.3 = (bf16[1,3,1024]{2,1,0:T(4,128)(2,1)S(1)}, bf16[1,3,1024]{2,1,0:T(4,128)(2,1)S(1)}, u32[]{:S(2)}, u32[]{:S(2)}) collective-permute-start(bf16[1,3,1024]{2,1,0:T(4,128)(2,1)S(1)} %slice.257), channel_id=1, source_target_pairs={{0,4},{4,8},{8,12},{1,5},{5,9},{9,13},{2,6},{6,10},{10,14},{3,7},{... | collective-permute-start | bytes 18440 | tf_op jit(solution)/shard_map/ppermute | solution.py:12
  25.8 5.0 %copy-start.19 = (f32[16,8,8,128]{3,2,1,0:T(8,128)}, f32[16,8,8,128]{3,2,1,0:T(8,128)S(1)}, u32[]{:S(2)}) copy-start(f32[16,8,8,128]{3,2,1,0:T(8,128)S(1)} %copy.137) | copy-start | bytes 1572868
  75.0 14.9 %collective-permute-start.1 = (f32[1,8,128,128]{3,2,1,0:T(8,128)}, f32[1,8,128,128]{3,2,1,0:T(8,128)S(1)}, u32[]{:S(2)}, u32[]{:S(2)}) collective-permute-start(f32[1,8,128,128]{3,2,1,0:T(8,128)} %fusion.559), channel_id=1, source_target_pairs={{4,0},{8,4},{12,8},{5,1},{9,5},{13,9},{6,2},{10,6},{14,10},{7,3},{... | collective-permute-start | bytes 1572872 | tf_op jit(solution)/shard_map/while/body/eval_jaxpr/ppermute | solution.py:12
  92.4 14.0 %collective-permute-start.1 = (f32[1,8,128,128]{3,2,1,0:T(8,128)}, f32[1,8,128,128]{3,2,1,0:T(8,128)S(1)}, u32[]{:S(2)}, u32[]{:S(2)}) collective-permute-start(f32[1,8,128,128]{3,2,1,0:T(8,128)} %fusion.559), channel_id=1, source_target_pairs={{4,0},{8,4},{12,8},{5,1},{9,5},{13,9},{6,2},{10,6},{14,10},{7,3},{... | collective-permute-start | bytes 1572872 | tf_op jit(solution)/shard_map/while/body/eval_jaxpr/ppermute | solution.py:12
  108.9 13.1 %collective-permute-start.1 = (f32[1,8,128,128]{3,2,1,0:T(8,128)}, f32[1,8,128,128]{3,2,1,0:T(8,128)S(1)}, u32[]{:S(2)}, u32[]{:S(2)}) collective-permute-start(f32[1,8,128,128]{3,2,1,0:T(8,128)} %fusion.559), channel_id=1, source_target_pairs={{4,0},{8,4},{12,8},{5,1},{9,5},{13,9},{6,2},{10,6},{14,10},{7,3},{... | collective-permute-start | bytes 1572872 | tf_op jit(solution)/shard_map/while/body/eval_jaxpr/ppermute | solution.py:12
  124.7 10.9 %collective-permute-start = (f32[1,8,128,128]{3,2,1,0:T(8,128)}, f32[1,8,128,128]{3,2,1,0:T(8,128)S(1)}, u32[]{:S(2)}, u32[]{:S(2)}) collective-permute-start(f32[1,8,128,128]{3,2,1,0:T(8,128)} %fusion.556), channel_id=1, source_target_pairs={{0,4},{4,8},{8,12},{1,5},{5,9},{9,13},{2,6},{6,10},{10,14},{3,7},{... | collective-permute-start | bytes 1572872 | tf_op jit(solution)/shard_map/while/body/eval_jaxpr/ppermute | solution.py:12
  138.1 11.5 %collective-permute-start = (f32[1,8,128,128]{3,2,1,0:T(8,128)}, f32[1,8,128,128]{3,2,1,0:T(8,128)S(1)}, u32[]{:S(2)}, u32[]{:S(2)}) collective-permute-start(f32[1,8,128,128]{3,2,1,0:T(8,128)} %fusion.556), channel_id=1, source_target_pairs={{0,4},{4,8},{8,12},{1,5},{5,9},{9,13},{2,6},{6,10},{10,14},{3,7},{... | collective-permute-start | bytes 1572872 | tf_op jit(solution)/shard_map/while/body/eval_jaxpr/ppermute | solution.py:12
  152.1 11.3 %collective-permute-start = (f32[1,8,128,128]{3,2,1,0:T(8,128)}, f32[1,8,128,128]{3,2,1,0:T(8,128)S(1)}, u32[]{:S(2)}, u32[]{:S(2)}) collective-permute-start(f32[1,8,128,128]{3,2,1,0:T(8,128)} %fusion.556), channel_id=1, source_target_pairs={{0,4},{4,8},{8,12},{1,5},{5,9},{9,13},{2,6},{6,10},{10,14},{3,7},{... | collective-permute-start | bytes 1572872 | tf_op jit(solution)/shard_map/while/body/eval_jaxpr/ppermute | solution.py:12
  217.3 2.8 copy-start.14
  218.5 2.8 copy-start.44
  249.8 2.8 copy-start.14
  250.9 2.8 copy-start.44
  296.5 8.3 %collective-permute-start.7 = (bf16[1,3,1024]{2,1,0:T(4,128)(2,1)S(1)}, bf16[1,3,1024]{2,1,0:T(4,128)(2,1)S(1)}, u32[]{:S(2)}, u32[]{:S(2)}) collective-permute-start(bf16[1,3,1024]{2,1,0:T(4,128)(2,1)S(1)} %slice.357), channel_id=1, source_target_pairs={{4,0},{8,4},{12,8},{5,1},{9,5},{13,9},{6,2},{10,6},{14,10},{7,3},{... | collective-permute-start | bytes 18440 | tf_op jit(solution)/shard_map/ppermute | solution.py:12
  299.6 4.0 %copy-start.93 = (f32[1,131,1024]{2,1,0:T(8,128)}, f32[1,131,1024]{2,1,0:T(8,128)S(1)}, u32[]{:S(2)}) copy-start(f32[1,131,1024]{2,1,0:T(8,128)S(1)} %pad_add_fusion.5) | copy-start | bytes 1609732
  299.6 4.0 %copy-start.87 = (f32[2,1,8,64,128]{4,3,2,1,0:T(8,128)S(1)}, f32[2,1,8,64,128]{4,3,2,1,0:T(8,128)}, u32[]{:S(2)}) copy-start(f32[2,1,8,64,128]{4,3,2,1,0:T(8,128)} %get-tuple-element.1377) | copy-start | bytes 1572868
  301.0 6.5 %collective-permute-start.6 = (bf16[1,3,1024]{2,1,0:T(4,128)(2,1)S(1)}, bf16[1,3,1024]{2,1,0:T(4,128)(2,1)S(1)}, u32[]{:S(2)}, u32[]{:S(2)}) collective-permute-start(bf16[1,3,1024]{2,1,0:T(4,128)(2,1)S(1)} %slice.358), channel_id=1, source_target_pairs={{4,0},{8,4},{12,8},{5,1},{9,5},{13,9},{6,2},{10,6},{14,10},{7,3},{... | collective-permute-start | bytes 18440 | tf_op jit(solution)/shard_map/ppermute | solution.py:12
  302.3 7.2 %collective-permute-start.5 = (bf16[1,3,1024]{2,1,0:T(4,128)(2,1)S(1)}, bf16[1,3,1024]{2,1,0:T(4,128)(2,1)S(1)}, u32[]{:S(2)}, u32[]{:S(2)}) collective-permute-start(bf16[1,3,1024]{2,1,0:T(4,128)(2,1)S(1)} %slice.359), channel_id=1, source_target_pairs={{4,0},{8,4},{12,8},{5,1},{9,5},{13,9},{6,2},{10,6},{14,10},{7,3},{... | collective-permute-start | bytes 18440 | tf_op jit(solution)/shard_map/ppermute | solution.py:12
  310.4 49.5 %copy-start.99 = (bf16[1,128,1024]{2,1,0:T(8,128)(2,1)}, bf16[1,128,1024]{2,1,0:T(8,128)(2,1)S(1)}, u32[]{:S(2)}) copy-start(bf16[1,128,1024]{2,1,0:T(8,128)(2,1)S(1)} %scatter-add.14) | copy-start | bytes 786436
  310.6 49.3 %copy-start.97 = (bf16[1,128,1024]{2,1,0:T(8,128)(2,1)}, bf16[1,128,1024]{2,1,0:T(8,128)(2,1)S(1)}, u32[]{:S(2)}) copy-start(bf16[1,128,1024]{2,1,0:T(8,128)(2,1)S(1)} %scatter-add.11) | copy-start | bytes 786436
  310.8 49.1 %copy-start.98 = (bf16[1,128,1024]{2,1,0:T(8,128)(2,1)}, bf16[1,128,1024]{2,1,0:T(8,128)(2,1)S(1)}, u32[]{:S(2)}) copy-start(bf16[1,128,1024]{2,1,0:T(8,128)(2,1)S(1)} %scatter-add.10) | copy-start | bytes 786436
  (165 other events, 188.9 us)
Sparse Core Ops, SparseCore 0:
  296.1 62.1 reduce-scatter.3
where the time goes:
time: 374 us; the launch traced here: 367 us
  matrix products  114 us (30%)
  waiting for transfers between devices  111 us (30%)
  local copies, waits for them, and re-layouts  76 us (20%)
  starting transfers between devices  31.1 us (8%)
  other arithmetic  16.3 us (4%)
  between operations  15.2 us (4%)
    ppermute x12, waiting for transfers between devices, from_behind(): return lax.ppermute(array, axis, pairs)  63.5 us
    unnamed x2, waiting for transfers between devices  47.6 us
    while x294, local copies, waits for them, and re-layouts  47.2 us
    ppermute x12, starting transfers between devices, from_behind(): return lax.ppermute(array, axis, pairs)  31.1 us
    dot_general x40, matrix products, solve_block(): jnp.einsum('...ij,...jk->...ik', power_term, power_term, precision=lax.Pr...  21.1 us
    dot_general x40, matrix products, solve_block(): jnp.einsum('...ij,...jk->...ik', inverse, eye_block + power_term, precisi...  20.7 us
    unnamed x70, local copies, waits for them, and re-layouts  12.5 us
    dot_general x3, matrix products, forward_hop(): jnp.einsum('...ij,...jk->...ik', transition, state_in, precision=lax.Prec...  7.54 us
  transfers between devices with their start and end apart: 13, of which 9 were waited for; matrix products, arithmetic and copies ran while one was open for 3% of the time, Pallas kernels for 0%

commit v1 on v0

v1 whole, which is shorter than its diff:
```python
import functools

import jax
import jax.numpy as jnp
from jax import lax
from jax.experimental import pallas as pl
from jax.experimental.pallas import tpu as pltpu
from jax.sharding import PartitionSpec as P

MESH = pl.DeviceIdType.MESH
F32 = jnp.float32
BF16 = jnp.bfloat16
SKEW = 2
GROUP = 4


def split(x):
    high = x.astype(BF16)
    return high, (x - high.astype(F32)).astype(BF16)


def whole(x):
    return x.astype(BF16), None


def mm(a, b, flip=False):
    ah, al = a
    bh, bl = b
    lhs = ah if al is None else jnp.concatenate([ah, al], axis=1)
    if flip:
        axis_n, axis_k = 0, 1
    else:
        axis_n, axis_k = 1, 0
    n = bh.shape[axis_n]
    rhs = bh if bl is None else jnp.concatenate([bh, bl], axis=axis_n)
    if al is not None:
        rhs = jnp.concatenate([rhs, rhs], axis=axis_k)
    out = lax.dot_general(
        lhs, rhs, (((1,), (axis_k,)), ((), ())), preferred_element_type=F32
    )
    if bl is not None:
        out = out[:, :n] + out[:, n:]
    return out


def kernel(
    shards, parts, scatter,
    q_raw, k_raw, v_raw, conv_ref, beta_ref, cot_ref,
    mixed_ref, dq_ref, dk_ref, dv_ref, dbeta_ref, conv_out,
    halo, q_s, k_s, v_s, g_s, p_s, gram_s, inv_s, wu_s, r_s, n_s, nt_s,
    out_state, out_adj, in_state, in_adj, edge_out, edge_in, tail, cg, cgt, gathered,
    halo_send, halo_recv, state_send, state_recv, adj_send, adj_recv,
    edge_send, edge_recv, cg_send, cg_recv,
):
    z = lax.axis_index("seq")
    heads = beta_ref.shape[0]
    count, width = q_raw.shape[0], q_raw.shape[1] // heads
    first, last = z == 0, z == shards - 1
    raws = (q_raw, k_raw, v_raw)
    grads = (dq_ref, dk_ref, dv_ref)

    barrier = pltpu.get_barrier_semaphore()
    if scatter:
        total = shards * parts
        mine = z * parts + lax.axis_index("dp")

        def peer_of(step):
            peer = lax.rem(mine + step, total)
            return peer, {"seq": peer // parts, "dp": lax.rem(peer, parts)}

        for step in range(1, total):
            pl.semaphore_signal(barrier, inc=1, device_id=peer_of(step)[1], device_id_type=MESH)
        pl.semaphore_wait(barrier, total - 1)
    else:
        @pl.when(z > 0)
        def _():
            pl.semaphore_signal(barrier, inc=1, device_id={"seq": z - 1}, device_id_type=MESH)

        @pl.when(z < shards - 1)
        def _():
            pl.semaphore_signal(barrier, inc=1, device_id={"seq": z + 1}, device_id_type=MESH)

        @pl.when(z > 0)
        def _():
            pl.semaphore_wait(barrier, 1)

        @pl.when(z < shards - 1)
        def _():
            pl.semaphore_wait(barrier, 1)

    def halo_copy(s):
        return pltpu.make_async_remote_copy(
            src_ref=raws[s].at[pl.ds(count - 16, 16), :], dst_ref=halo.at[s],
            send_sem=halo_send.at[s], recv_sem=halo_recv.at[s],
            device_id={"seq": z + 1}, device_id_type=MESH,
        )

    def state_copy(h):
        return pltpu.make_async_remote_copy(
            src_ref=out_state.at[h], dst_ref=in_state.at[h],
            send_sem=state_send.at[h], recv_sem=state_recv.at[h],
            device_id={"seq": z + 1}, device_id_type=MESH,
        )

    def adj_copy(h):
        return pltpu.make_async_remote_copy(
            src_ref=out_adj.at[h], dst_ref=in_adj.at[h],
            send_sem=adj_send.at[h], recv_sem=adj_recv.at[h],
            device_id={"seq": z - 1}, device_id_type=MESH,
        )

    def edge_copy(h):
        return pltpu.make_async_remote_copy(
            src_ref=edge_out.at[h], dst_ref=edge_in.at[h],
            send_sem=edge_send.at[h], recv_sem=edge_recv.at[h],
            device_id={"seq": z - 1}, device_id_type=MESH,
        )

    @pl.when(z < shards - 1)
    def _():
        for s in range(3):
            halo_copy(s).start()

    @pl.when(first)
    def _():
        halo[...] = jnp.zeros_like(halo)
        in_state[...] = jnp.zeros_like(in_state)

    @pl.when(last)
    def _():
        in_adj[...] = jnp.zeros_like(in_adj)
        edge_in[...] = jnp.zeros_like(edge_in)

    cg[...] = jnp.zeros_like(cg)
    rows = lax.broadcasted_iota(jnp.int32, (count, count), 0)
    cols = lax.broadcasted_iota(jnp.int32, (count, count), 1)
    apart = rows ^ cols
    strict = rows > cols
    lower = rows >= cols
    eye = rows == cols

    def beta_of(h):
        row = 1.0 / (1.0 + jnp.exp(-beta_ref[pl.ds(h, 1), :]))
        return row, jnp.sum(jnp.where(eye, row, 0.0), axis=1, keepdims=True)

    def lanes_of(h):
        return pl.ds(pl.multiple_of(h * width, width), width)

    def series_of(s, h):
        before = halo[s, :, lanes_of(h)].astype(F32)[8:]
        return jnp.concatenate([before, raws[s][:, lanes_of(h)].astype(F32)], axis=0)

    @pl.when(z > 0)
    def _():
        for s in range(3):
            halo_copy(s).wait_recv()

    def prepare(step, carry):
        ids = [step * GROUP + i for i in range(GROUP)]
        qs, ks, vs = [], [], []
        for h in ids:
            lanes = lanes_of(h)
            made = []
            for s in range(3):
                ext = series_of(s, h)
                pre = conv_ref[pl.ds(s * 4, 1), lanes] * ext[5:5 + count]
                for j in range(1, 4):
                    pre = pre + conv_ref[pl.ds(s * 4 + j, 1), lanes] * ext[5 + j:5 + j + count]
                gate = 1.0 / (1.0 + jnp.exp(-pre))
                act = pre * gate
                slope = gate * (1.0 + pre * (1.0 - gate))
                if s < 2:
                    scale = lax.rsqrt(jnp.sum(act * act, axis=1, keepdims=True) + 1e-06)
                    act = act * scale
                    slope = slope * scale
                g_s[s, h] = slope
                made.append(act)
            q_s[h], k_s[h], v_s[h] = made
            qs.append(made[0])
            ks.append(made[1])
            vs.append(made[2])
        k2 = [split(k) for k in ks]
        gram = [mm(k, k, True) for k in k2]
        score = [jnp.where(lower, mm(split(q), k, True), 0.0) for q, k in zip(qs, k2)]
        betas = [beta_of(h) for h in ids]
        low = [jnp.where(strict, b[1] * g, 0.0) for b, g in zip(betas, gram)]
        inv = [jnp.where(eye, 1.0, 0.0) - jnp.where(apart < 2, a, 0.0) for a in low]
        size = 2
        while size < count:
            band = (apart >= size) & (apart < 2 * size)
            i2 = [split(m) for m in inv]
            part = [mm(split(jnp.where(band, a, 0.0)), m) for a, m in zip(low, i2)]
            inv = [m - mm(n, split(x)) for m, n, x in zip(inv, i2, part)]
            size *= 2
        wu = [
            mm(split(m * b[0]), split(jnp.concatenate([k, v], axis=1)))
            for m, b, k, v in zip(inv, betas, ks, vs)
        ]
        nb = [mm(split(k.T), split(x)) for k, x in zip(ks, wu)]
        reader = [q - mm(split(p), split(x[:, :width])) for q, p, x in zip(qs, score, wu)]
        source = [
            mm(split(r.T), (cot_ref[:, lanes_of(h)], None)) for r, h in zip(reader, ids)
        ]
        for i, h in enumerate(ids):
            out_state[h] = nb[i][:, width:]
            out_adj[h] = source[i]
            p_s[h] = score[i]
            gram_s[h] = gram[i]
            inv_s[h] = inv[i]
            wu_s[h] = wu[i]
            r_s[h] = reader[i]
            n_s[h] = jnp.concatenate(split(nb[i][:, :width]), axis=1)
            nt_s[h] = jnp.concatenate(split(nb[i][:, :width].T), axis=1)

        @pl.when(first)
        def _():
            for h in ids:
                state_copy(h).start()

        @pl.when(last)
        def _():
            for h in ids:
                adj_copy(h).start()

        return carry

    lax.fori_loop(0, heads // GROUP, prepare, 0)

    def advance(pair, value):
        high, low = split(value)
        both = jnp.concatenate([high, low], axis=1)
        out = jnp.dot(pair, jnp.concatenate([both, both], axis=0), preferred_element_type=F32)
        return value - (out[:, :width] + out[:, width:])

    def finish(h):
        lanes = lanes_of(h)
        cot = cot_ref[:, lanes]
        query, key, value = q_s[h], k_s[h], v_s[h]
        score, wu, reader = p_s[h], wu_s[h], r_s[h]
        w_rows, u_rows = wu[:, :width], wu[:, width:]
        state2, adj2 = split(in_state[h]), split(in_adj[h])
        key2 = split(key)
        beta_row, beta_col = beta_of(h)
        reads = mm(split(jnp.concatenate([w_rows, reader], axis=0)), state2)
        corrected = u_rows - reads[:count]
        mixed_ref[:, lanes] = reads[count:] + mm(split(score), split(u_rows))
        d_corr = mm(split(score.T), (cot, None)) + mm(key2, adj2)
        corr2 = split(corrected)
        d_score = jnp.where(lower, mm((cot, None), corr2, True), 0.0)
        back = mm(split(jnp.concatenate([cot.astype(F32), d_corr], axis=0)), state2, True)
        y = mm(split(inv_s[h].T), split(jnp.concatenate([-back[count:], d_corr], axis=1)))
        y_k, y_v = y[:, :width], y[:, width:]
        d_low = jnp.where(strict, -mm(split(y), split(wu), True), 0.0)
        d_beta = jnp.sum(y_k * key + y_v * value + d_low * gram_s[h], axis=1, keepdims=True)
        d_gram = beta_col * d_low
        onto = mm(split(jnp.concatenate([d_score, d_gram + d_gram.T], axis=0)), key2)
        d_query = back[:count] + onto[:count]
        d_key = (
            mm(split(d_score.T), split(query)) + mm(corr2, adj2, True)
            + beta_col * y_k + onto[count:]
        )
        d_value = beta_col * y_v
        d_row = jnp.sum(jnp.where(eye, d_beta, 0.0), axis=0, keepdims=True)
        dbeta_ref[pl.ds(h, 1), :] = d_row * beta_row * (1.0 - beta_row)
        blank = jnp.zeros((8, width), F32)
        for s, grad in enumerate((d_query, d_key, d_value)):
            if s < 2:
                unit = (query, key)[s]
                grad = grad - unit * jnp.sum(grad * unit, axis=1, keepdims=True)
            d_pre = grad * g_s[s, h]
            ext = jnp.concatenate([blank, d_pre, blank], axis=0)
            series = series_of(s, h)
            full = None
            for j in range(4):
                moved = ext[3 - j:3 - j + count + 8]
                term = conv_ref[pl.ds(s * 4 + j, 1), lanes] * moved
                full = term if full is None else full + term
                cg[pl.ds((s * 4 + j) * heads + h, 1), :] = jnp.sum(
                    series * moved, axis=0, keepdims=True
                )
            edge_out[h, s * 8:s * 8 + 8, :] = full[:8]
            grads[s][:, lanes] = full[8:].astype(BF16)
            tail[h, s * 8:s * 8 + 8, :] = full[count:]

        @pl.when(z > 0)
        def _():
            edge_copy(h).start()

    early = z < shards // 2
    lag_state = jnp.where(early, 0, SKEW)
    lag_adj = jnp.where(early, SKEW, 0)

    def chain(step, carry):
        hs = step - lag_state
        ha = step - lag_adj

        @pl.when((hs >= 0) & (hs < heads) & (z > 0))
        def _():
            state_copy(hs).wait_recv()

            @pl.when(z < shards - 1)
            def _():
                out_state[hs] = out_state[hs] + advance(n_s[hs], in_state[hs])
                state_copy(hs).start()

        @pl.when((ha >= 0) & (ha < heads) & (z < shards - 1))
        def _():
            adj_copy(ha).wait_recv()

            @pl.when(z > 0)
            def _():
                out_adj[ha] = out_adj[ha] + advance(nt_s[ha], in_adj[ha])
                adj_copy(ha).start()

        @pl.when(step >= SKEW)
        def _():
            finish(step - SKEW)

        return carry

    lax.fori_loop(0, heads + SKEW, chain, 0)

    if scatter:
        piece = cgt.shape[0] // total
        cgt[...] = cg[...].T

        def cg_copy(step):
            peer, where = peer_of(step)
            return pltpu.make_async_remote_copy(
                src_ref=cgt.at[pl.ds(pl.multiple_of(peer * piece, 8), piece), :],
                dst_ref=gathered.at[step],
                send_sem=cg_send.at[step], recv_sem=cg_recv.at[step],
                device_id=where, device_id_type=MESH,
            )

        for step in range(1, total):
            cg_copy(step).start()

    @pl.when(z < shards - 1)
    def _():
        def take(h, carry):
            edge_copy(h).wait_recv()
            return carry

        lax.fori_loop(0, heads, take, 0)

    for h in range(heads):
        for s in range(3):
            lanes = slice(h * width, (h + 1) * width)
            extra = tail[h, s * 8:s * 8 + 8, :] + edge_in[h, s * 8:s * 8 + 8, :]
            grads[s][count - 8:, lanes] = extra.astype(BF16)

    if scatter:
        sums = cgt[pl.ds(pl.multiple_of(mine * piece, 8), piece), :]
        for step in range(1, total):
            cg_copy(step).wait_recv()
            sums = sums + gathered[step]
        conv_out[...] = sums
        for step in range(1, total):
            cg_copy(step).wait_send()
    else:
        conv_out[...] = cg[...]

    @pl.when(z < shards - 1)
    def _():
        for s in range(3):
            halo_copy(s).wait_send()

        def sent(h, carry):
            state_copy(h).wait_send()
            return carry

        lax.fori_loop(0, heads, sent, 0)

    @pl.when(z > 0)
    def _():
        def sent(h, carry):
            adj_copy(h).wait_send()
            edge_copy(h).wait_send()
            return carry

        lax.fori_loop(0, heads, sent, 0)


def per_device(query_raw, key_raw, value_raw, conv_weight, beta_logit, cotangent):
    shards, parts = lax.axis_size("seq"), lax.axis_size("dp")
    heads = beta_logit.shape[1]
    count, channels = query_raw.shape[1:]
    width = channels // heads
    taps = conv_weight.shape[1]
    total = shards * parts
    scatter = total > 1 and width % (8 * total) == 0
    piece = width // total if scatter else 8
    slots = total if scatter else 2
    square = lambda dtype=F32, cols=width: pltpu.VMEM((heads, count, cols), dtype)
    dma = pltpu.SemaphoreType.DMA
    vmem = pl.BlockSpec(memory_space=pltpu.VMEM)
    conv_rows = piece if scatter else width
    outs = pl.pallas_call(
        functools.partial(kernel, shards, parts, scatter),
        out_shape=(
            jax.ShapeDtypeStruct((count, channels), F32),
            jax.ShapeDtypeStruct((count, channels), BF16),
            jax.ShapeDtypeStruct((count, channels), BF16),
            jax.ShapeDtypeStruct((count, channels), BF16),
            jax.ShapeDtypeStruct((heads, count), F32),
            jax.ShapeDtypeStruct((conv_rows, 128), F32),
        ),
        in_specs=[vmem] * 6,
        out_specs=[vmem] * 6,
        scratch_shapes=[
            pltpu.VMEM((3, 16, channels), BF16),
            square(), square(), square(),
            pltpu.VMEM((3, heads, count, width), F32),
            square(), square(), square(), square(F32, 2 * width), square(),
            square(BF16, 2 * width), square(BF16, 2 * width),
            square(), square(), square(), square(),
            pltpu.VMEM((heads, 24, width), F32),
            pltpu.VMEM((heads, 24, width), F32),
            pltpu.VMEM((heads, 24, width), F32),
            pltpu.VMEM((128, width), F32),
            pltpu.VMEM((width, 128), F32),
            pltpu.VMEM((slots, piece, 128), F32),
            dma((3,)), dma((3,)),
            dma((heads,)), dma((heads,)), dma((heads,)), dma((heads,)),
            dma((heads,)), dma((heads,)), dma((slots,)), dma((slots,)),
        ],
        compiler_params=pltpu.CompilerParams(
            collective_id=0, has_side_effects=True, vmem_limit_bytes=48 << 20
        ),
    )(
        query_raw[0], key_raw[0], value_raw[0],
        conv_weight.reshape(3 * taps, channels), beta_logit[0], cotangent[0],
    )
    mixed, d_query, d_key, d_value, d_beta, conv = outs
    used = 3 * taps * heads
    if scatter:
        conv_grad = conv[:, :used].T.reshape(3, taps, heads, piece)
    else:
        conv_grad = lax.psum_scatter(
            conv[:used].reshape(3, taps, heads, width),
            ("seq", "dp"), scatter_dimension=3, tiled=True,
        )
    return (mixed[None], d_query[None], d_key[None], d_value[None], d_beta[None], conv_grad)


def solution(mesh):
    rows = P(("group", "dp"), "seq", "head")
    in_specs = (
        rows, rows, rows,
        P(None, None, "head"),
        P(("group", "dp"), "head", "seq"),
        rows,
    )
    out_specs = (
        rows, rows, rows, rows,
        P(("group", "dp"), "head", "seq"),
        P("group", None, "head", ("seq", "dp")),
    )
    return jax.shard_map(
        per_device, mesh=mesh, in_specs=in_specs, out_specs=out_specs, check_vma=False
    )
```

time: 374 us -> 53 us (0.14); the launches traced: 367 us -> 52.7 us
  matrix products: 114 us -> 0 us
  waiting for transfers between devices: 111 us -> 0 us
  local copies, waits for them, and re-layouts: 76 us -> 8.83 us
  Pallas kernels: 0 us -> 43.2 us
  starting transfers between devices: 31.1 us -> 0 us
  other arithmetic: 16.3 us -> 0 us
  between operations: 15.2 us -> 0.68 us
    dot_general x150 -> x0, matrix products: 114 us -> none  [the longest x40 21.1 us: solve_block(): jnp.einsum('...ij,...jk->...ik', power_term, power_term, precision=lax.Pr...]
    ppermute x12 -> x0, waiting for transfers between devices: 63.5 us -> none  [from_behind(): return lax.ppermute(array, axis, pairs)]
    while x295 -> x0, local copies, waits for them, and re-layouts: 48.3 us -> none
    unnamed x2 -> x0, waiting for transfers between devices: 47.6 us -> none
    pallas_call x0 -> x1, Pallas kernels: none -> 43.2 us  [per_device(): pl.pallas_call(functools.partial(kernel, shards, parts, scatter), out_sha...]
    ppermute x12 -> x0, starting transfers between devices: 31.1 us -> none  [from_behind(): return lax.ppermute(array, axis, pairs)]
    another operation x9 -> x0, local copies, waits for them, and re-layouts: 6.05 us -> none
    unnamed x70 -> x15, local copies, waits for them, and re-layouts: 12.5 us -> 7.29 us
  transfers between devices with their start and end apart: 13 -> 0, of which waited for: 9 -> 0; matrix products, arithmetic and copies ran while one was open for 3% -> 0% of each run, Pallas kernels for 0% -> 0%
where the time goes in v1:
time: 53 us; the launch traced here: 52.7 us
  Pallas kernels  43.2 us (82%)
  local copies, waits for them, and re-layouts  8.83 us (17%)
  between operations  0.68 us (1%)
    pallas_call x1, Pallas kernels, per_device(): pl.pallas_call(functools.partial(kernel, shards, parts, scatter), out_sha...  43.2 us
    unnamed x15, local copies, waits for them, and re-layouts  7.29 us

profile of v1, /device:TPU:0, one launch (start us, length us, event | category | flops | bytes accessed | tf_op | source)
XLA Modules:
  0.0 52.7 jit_solution(4295477947110484623)
XLA Ops:
  0.6 0.0 copy-start.4
  0.6 0.8 %reshape.18.conv_ref = f32[12,1024]{1,0:T(8,128)S(1)} reshape(f32[3,4,1024]{2,1,0:T(4,128)} %param.9) | data formatting | bytes 98304 | tf_op jit(solution)/shard_map/reshape | solution.py:433
  1.5 0.0 copy-done.4
  1.5 0.0 copy-start
  1.5 0.9 %copy-done = bf16[1,128,1024]{2,1,0:T(8,128)(2,1)S(1)} copy-done((bf16[1,128,1024]{2,1,0:T(8,128)(2,1)S(1)}, bf16[1,128,1024]{2,1,0:T(8,128)(2,1)}, u32[]{:S(2)}) %copy-start) | copy-done | bytes 262168
  2.4 0.0 copy-start.1
  2.4 0.9 %copy-done.1 = bf16[1,128,1024]{2,1,0:T(8,128)(2,1)S(1)} copy-done((bf16[1,128,1024]{2,1,0:T(8,128)(2,1)S(1)}, bf16[1,128,1024]{2,1,0:T(8,128)(2,1)}, u32[]{:S(2)}) %copy-start.1) | copy-done | bytes 262168
  3.4 0.0 copy-start.2
  3.4 0.9 %copy-done.2 = bf16[1,128,1024]{2,1,0:T(8,128)(2,1)S(1)} copy-done((bf16[1,128,1024]{2,1,0:T(8,128)(2,1)S(1)}, bf16[1,128,1024]{2,1,0:T(8,128)(2,1)}, u32[]{:S(2)}) %copy-start.2) | copy-done | bytes 262168
  4.3 0.0 copy-start.3
  4.3 0.9 %copy-done.3 = bf16[1,128,1024]{2,1,0:T(8,128)(2,1)S(1)} copy-done((bf16[1,128,1024]{2,1,0:T(8,128)(2,1)S(1)}, bf16[1,128,1024]{2,1,0:T(8,128)(2,1)}, u32[]{:S(2)}) %copy-start.3) | copy-done | bytes 262168
  5.3 43.2 %shard_map.109 = (f32[128,1024]{1,0:T(8,128)S(1)}, bf16[128,1024]{1,0:T(8,128)(2,1)S(1)}, bf16[128,1024]{1,0:T(8,128)(2,1)S(1)}, bf16[128,1024]{1,0:T(8,128)(2,1...) custom-call(bf16[128,1024]{1,0:T(8,128)(2,1)S(1)} %bitcast.14, bf16[128,1024]{1,0:T(8,128)(2,1)S(1)} %bitcast.15, ...), custom_call_target="tpu_custom_call" | custom-call | tf_op jit(solution)/shard_map/pallas_call | solution.py:399
  48.5 0.7 %copy.13 = f32[96,16]{1,0:T(8,128)} copy(f32[96,16]{0,1:T(8,128)S(1)} %slice_bitcast_fusion) | data formatting | bytes 12288 | tf_op jit(solution)/shard_map/transpose | solution.py:438
  49.2 0.8 %copy.19 = f32[1,128,1024]{2,1,0:T(8,128)} copy(f32[1,128,1024]{2,1,0:T(8,128)S(1)} %bitcast.13) | data formatting | bytes 1048576
  50.0 0.7 %copy.20 = bf16[1,128,1024]{2,1,0:T(8,128)(2,1)} copy(bf16[1,128,1024]{2,1,0:T(8,128)(2,1)S(1)} %bitcast.20) | data formatting | bytes 524288
  50.7 0.7 %copy.21 = bf16[1,128,1024]{2,1,0:T(8,128)(2,1)} copy(bf16[1,128,1024]{2,1,0:T(8,128)(2,1)S(1)} %bitcast.19) | data formatting | bytes 524288
  51.4 0.7 %copy.22 = bf16[1,128,1024]{2,1,0:T(8,128)(2,1)} copy(bf16[1,128,1024]{2,1,0:T(8,128)(2,1)S(1)} %bitcast.18) | data formatting | bytes 524288
  52.1 0.6 %copy.23 = f32[1,8,128]{2,1,0:T(8,128)} copy(f32[1,8,128]{2,1,0:T(8,128)S(1)} %bitcast.22) | data formatting | bytes 8192
  (1 shorter events, 0.0 us)
Async XLA Ops:
  0.6 0.8 %copy-start.4 = (f32[1,8,128]{2,1,0:T(8,128)S(1)}, f32[1,8,128]{2,1,0:T(8,128)}, u32[]{:S(2)}) copy-start(f32[1,8,128]{2,1,0:T(8,128)} %param.10) | copy-start | bytes 12292
  1.5 1.0 %copy-start = (bf16[1,128,1024]{2,1,0:T(8,128)(2,1)S(1)}, bf16[1,128,1024]{2,1,0:T(8,128)(2,1)}, u32[]{:S(2)}) copy-start(bf16[1,128,1024]{2,1,0:T(8,128)(2,1)} %param.6) | copy-start | bytes 786436
  2.4 0.9 %copy-start.1 = (bf16[1,128,1024]{2,1,0:T(8,128)(2,1)S(1)}, bf16[1,128,1024]{2,1,0:T(8,128)(2,1)}, u32[]{:S(2)}) copy-start(bf16[1,128,1024]{2,1,0:T(8,128)(2,1)} %param.7) | copy-start | bytes 786436
  3.4 0.9 %copy-start.2 = (bf16[1,128,1024]{2,1,0:T(8,128)(2,1)S(1)}, bf16[1,128,1024]{2,1,0:T(8,128)(2,1)}, u32[]{:S(2)}) copy-start(bf16[1,128,1024]{2,1,0:T(8,128)(2,1)} %param.8) | copy-start | bytes 786436
  4.3 0.9 %copy-start.3 = (bf16[1,128,1024]{2,1,0:T(8,128)(2,1)S(1)}, bf16[1,128,1024]{2,1,0:T(8,128)(2,1)}, u32[]{:S(2)}) copy-start(bf16[1,128,1024]{2,1,0:T(8,128)(2,1)} %param.11) | copy-start | bytes 786436

commit v2 on v1

--- a/solution.py
+++ b/solution.py
@@ -45,52 +45,69 @@
 
 def kernel(
     shards, parts, scatter,
+    q_hbm, k_hbm, v_hbm, conv_hbm, beta_hbm, cot_hbm,
+    mixed_ref, dq_ref, dk_ref, dv_ref, dbeta_ref, conv_out,
     q_raw, k_raw, v_raw, conv_ref, beta_ref, cot_ref,
-    mixed_ref, dq_ref, dk_ref, dv_ref, dbeta_ref, conv_out,
     halo, q_s, k_s, v_s, g_s, p_s, gram_s, inv_s, wu_s, r_s, n_s, nt_s,
     out_state, out_adj, in_state, in_adj, edge_out, edge_in, tail, cg, cgt, gathered,
     halo_send, halo_recv, state_send, state_recv, adj_send, adj_recv,
-    edge_send, edge_recv, cg_send, cg_recv,
+    edge_send, edge_recv, cg_send, cg_recv, load_sem, beside,
 ):
     z = lax.axis_index("seq")
     heads = beta_ref.shape[0]
     count, width = q_raw.shape[0], q_raw.shape[1] // heads
     first, last = z == 0, z == shards - 1
     raws = (q_raw, k_raw, v_raw)
+    sources = (q_hbm, k_hbm, v_hbm, conv_hbm, beta_hbm, cot_hbm)
+    loads = [
+        pltpu.make_async_copy(source, kept, load_sem.at[i])
+        for i, (source, kept) in enumerate(
+            zip(sources, (q_raw, k_raw, v_raw, conv_ref, beta_ref, cot_ref))
+        )
+    ]
+    for load in loads:
+        load.start()
     grads = (dq_ref, dk_ref, dv_ref)
 
     barrier = pltpu.get_barrier_semaphore()
     if scatter:
         total = shards * parts
-        mine = z * parts + lax.axis_index("dp")
+        column = lax.axis_index("dp")
+        mine = z * parts + column
 
         def peer_of(step):
             peer = lax.rem(mine + step, total)
             return peer, {"seq": peer // parts, "dp": lax.rem(peer, parts)}
 
-        for step in range(1, total):
-            pl.semaphore_signal(barrier, inc=1, device_id=peer_of(step)[1], device_id_type=MESH)
-        pl.semaphore_wait(barrier, total - 1)
-    else:
-        @pl.when(z > 0)
-        def _():
-            pl.semaphore_signal(barrier, inc=1, device_id={"seq": z - 1}, device_id_type=MESH)
-
-        @pl.when(z < shards - 1)
-        def _():
-            pl.semaphore_signal(barrier, inc=1, device_id={"seq": z + 1}, device_id_type=MESH)
-
-        @pl.when(z > 0)
-        def _():
-            pl.semaphore_wait(barrier, 1)
-
-        @pl.when(z < shards - 1)
-        def _():
-            pl.semaphore_wait(barrier, 1)
+        def beside_of(step):
+            return {"dp": lax.rem(column + step, parts)}
+
+        for step in range(1, parts):
+            pl.semaphore_signal(
+                barrier, inc=1, device_id=beside_of(step), device_id_type=MESH
+            )
+
+    @pl.when(z > 0)
+    def _():
+        pl.semaphore_signal(barrier, inc=1, device_id={"seq": z - 1}, device_id_type=MESH)
+
+    @pl.when(z < shards - 1)
+    def _():
+        pl.semaphore_signal(barrier, inc=1, device_id={"seq": z + 1}, device_id_type=MESH)
+
+    met = parts - 1 if scatter else 0
+
+    @pl.when((z > 0) & (z < shards - 1))
+    def _():
+        pl.semaphore_wait(barrier, met + 2)
+
+    @pl.when(first | last)
+    def _():
+        pl.semaphore_wait(barrier, met + 1)
 
     def halo_copy(s):
         return pltpu.make_async_remote_copy(
-            src_ref=raws[s].at[pl.ds(count - 16, 16), :], dst_ref=halo.at[s],
+            src_ref=sources[s].at[pl.ds(count - 16, 16), :], dst_ref=halo.at[s],
             send_sem=halo_send.at[s], recv_sem=halo_recv.at[s],
             device_id={"seq": z + 1}, device_id_type=MESH,
         )
@@ -149,6 +166,9 @@
     def series_of(s, h):
         before = halo[s, :, lanes_of(h)].astype(F32)[8:]
         return jnp.concatenate([before, raws[s][:, lanes_of(h)].astype(F32)], axis=0)
+
+    for load in loads:
+        load.wait()
 
     @pl.when(z > 0)
     def _():
@@ -163,9 +183,9 @@
             made = []
             for s in range(3):
                 ext = series_of(s, h)
-                pre = conv_ref[pl.ds(s * 4, 1), lanes] * ext[5:5 + count]
+                pre = conv_ref[s, 0:1, lanes] * ext[5:5 + count]
                 for j in range(1, 4):
-                    pre = pre + conv_ref[pl.ds(s * 4 + j, 1), lanes] * ext[5 + j:5 + j + count]
+                    pre = pre + conv_ref[s, j:j + 1, lanes] * ext[5 + j:5 + j + count]
                 gate = 1.0 / (1.0 + jnp.exp(-pre))
                 act = pre * gate
                 slope = gate * (1.0 + pre * (1.0 - gate))
@@ -273,7 +293,7 @@
             full = None
             for j in range(4):
                 moved = ext[3 - j:3 - j + count + 8]
-                term = conv_ref[pl.ds(s * 4 + j, 1), lanes] * moved
+                term = conv_ref[s, j:j + 1, lanes] * moved
                 full = term if full is None else full + term
                 cg[pl.ds((s * 4 + j) * heads + h, 1), :] = jnp.sum(
                     series * moved, axis=0, keepdims=True
@@ -316,11 +336,21 @@
         def _():
             finish(step - SKEW)
 
+        if scatter:
+            @pl.when(step == SKEW)
+            def _():
+                for other in range(1, parts):
+                    pl.semaphore_signal(
+                        beside, inc=1, device_id=beside_of(other), device_id_type=MESH
+                    )
+
         return carry
 
     lax.fori_loop(0, heads + SKEW, chain, 0)
 
     if scatter:
+        if parts > 1:
+            pl.semaphore_wait(beside, parts - 1)
         piece = cgt.shape[0] // total
         cgt[...] = cg[...].T
 
@@ -380,6 +410,27 @@
             return carry
 
         lax.fori_loop(0, heads, sent, 0)
+
+
+def flush(count, *refs):
+    blocks, rest = refs[:count], refs[count:]
+    if len(rest) == count + 1:
+        outs, sems = rest[:count], rest[count]
+        extra = ()
+    else:
+        conv, outs, conv_out, sems, turned = rest[0], rest[1:count + 1], *rest[count + 1:]
+        extra = ((turned, conv_out),)
+    copies = [
+        pltpu.make_async_copy(block, out, sems.at[i])
+        for i, (block, out) in enumerate((*zip(blocks, outs), *extra))
+    ]
+    for copy in copies[:count]:
+        copy.start()
+    if extra:
+        turned[...] = conv[...].T[:turned.shape[0]]
+        copies[count].start()
+    for copy in copies:
+        copy.wait()
 
 
 def per_device(query_raw, key_raw, value_raw, conv_weight, beta_logit, cotangent):
@@ -406,9 +457,15 @@
             jax.ShapeDtypeStruct((heads, count), F32),
             jax.ShapeDtypeStruct((conv_rows, 128), F32),
         ),
-        in_specs=[vmem] * 6,
+        in_specs=[pl.BlockSpec(memory_space=pltpu.HBM)] * 6,
         out_specs=[vmem] * 6,
         scratch_shapes=[
+            pltpu.VMEM((count, channels), BF16),
+            pltpu.VMEM((count, channels), BF16),
+            pltpu.VMEM((count, channels), BF16),
+            pltpu.VMEM((3, taps, channels), F32),
+            pltpu.VMEM((heads, count), F32),
+            pltpu.VMEM((count, channels), BF16),
             pltpu.VMEM((3, 16, channels), BF16),
             square(), square(), square(),
             pltpu.VMEM((3, heads, count, width), F32),
@@ -423,19 +480,39 @@
             pltpu.VMEM((slots, piece, 128), F32),
             dma((3,)), dma((3,)),
             dma((heads,)), dma((heads,)), dma((heads,)), dma((heads,)),
-            dma((heads,)), dma((heads,)), dma((slots,)), dma((slots,)),
+            dma((heads,)), dma((heads,)), dma((slots,)), dma((slots,)), dma((6,)),
+            pltpu.SemaphoreType.REGULAR,
         ],
         compiler_params=pltpu.CompilerParams(
             collective_id=0, has_side_effects=True, vmem_limit_bytes=48 << 20
         ),
     )(
-        query_raw[0], key_raw[0], value_raw[0],
-        conv_weight.reshape(3 * taps, channels), beta_logit[0], cotangent[0],
+        *(
+            pltpu.with_memory_space_constraint(x, pltpu.HBM)
+            for x in (
+                query_raw[0], key_raw[0], value_raw[0],
+                conv_weight, beta_logit[0], cotangent[0],
+            )
+        )
     )
-    mixed, d_query, d_key, d_value, d_beta, conv = outs
     used = 3 * taps * heads
+    blocks, conv = outs[:5], outs[5]
+    held, free = pl.BlockSpec(memory_space=pl.ANY), pl.BlockSpec(memory_space=pltpu.HBM)
+    extra_shape = (jax.ShapeDtypeStruct((used, piece), F32),) if scatter else ()
+    flushed = pl.pallas_call(
+        functools.partial(flush, 5),
+        out_shape=(*(jax.ShapeDtypeStruct(x.shape, x.dtype) for x in blocks), *extra_shape),
+        in_specs=[held] * 5 + [vmem] * len(extra_shape),
+        out_specs=[free] * (5 + len(extra_shape)),
+        scratch_shapes=[
+            dma((5 + len(extra_shape),)),
+            *(pltpu.VMEM(x.shape, F32) for x in extra_shape),
+        ],
+        compiler_params=pltpu.CompilerParams(vmem_limit_bytes=2 << 20),
+    )(*blocks, *((conv,) if scatter else ()))
+    mixed, d_query, d_key, d_value, d_beta = flushed[:5]
     if scatter:
-        conv_grad = conv[:, :used].T.reshape(3, taps, heads, piece)
+        conv_grad = flushed[5].reshape(3, taps, heads, piece)
     else:
         conv_grad = lax.psum_scatter(
             conv[:used].reshape(3, taps, heads, width),

time: 53 us -> 44.1 us (0.83)
  local copies, waits for them, and re-layouts: 8.83 us -> 0 us
    unnamed x15 -> x0, local copies, waits for them, and re-layouts: 7.29 us -> none
    pallas_call x0 -> x1, Pallas kernels: none -> 1.11 us  [per_device(): pl.pallas_call(functools.partial(flush, 5), out_shape=(*(jax.ShapeDtypeSt...]
    pallas_call x1, Pallas kernels: 43.2 us -> 42.2 us  [per_device(): pl.pallas_call(functools.partial(kernel, shards, parts, scatter), out_sha...]
    reshape x1 -> x0, local copies, waits for them, and re-layouts: 0.82 us -> none  [per_device(): conv_weight.reshape(3 * taps, channels)]
    transpose x2 -> x0, local copies, waits for them, and re-layouts: 0.71 us -> none  [per_device(): conv_grad = conv[:, :used].T.reshape(3, taps, heads, piece)]
where the time goes in v2:
time: 44.1 us; the launch traced here: 43.9 us
  Pallas kernels  43.3 us (98%)
  between operations  0.64 us (1%)
    pallas_call x1, Pallas kernels, per_device(): pl.pallas_call(functools.partial(kernel, shards, parts, scatter), out_sha...  42.2 us
    pallas_call x1, Pallas kernels, per_device(): pl.pallas_call(functools.partial(flush, 5), out_shape=(*(jax.ShapeDtypeSt...  1.11 us

profile of v2, /device:TPU:0, one launch (start us, length us, event | category | flops | bytes accessed | tf_op | source)
XLA Modules:
  0.0 43.9 jit_solution(5646568157554847918)
XLA Ops:
  0.6 42.2 %shard_map.109 = (f32[128,1024]{1,0:T(8,128)S(1)}, bf16[128,1024]{1,0:T(8,128)(2,1)S(1)}, bf16[128,1024]{1,0:T(8,128)(2,1)S(1)}, bf16[128,1024]{1,0:T(8,128)(2,1...) custom-call(bf16[128,1024]{1,0:T(8,128)(2,1)} %bitcast.11, bf16[128,1024]{1,0:T(8,128)(2,1)} %bitcast.12, ...), custom_call_target="tpu_custom_call" | custom-call | tf_op jit(solution)/shard_map/pallas_call | solution.py:450
  42.8 1.1 %shard_map.110 = (f32[128,1024]{1,0:T(8,128)}, bf16[128,1024]{1,0:T(8,128)(2,1)}, bf16[128,1024]{1,0:T(8,128)(2,1)}, bf16[128,1024]{1,0:T(8,128)(2,1)}, f32[8,128]{1,0:T(8,128)}, /*index=5*/f32[96,16]{1,0:T(8,128)}) custom-call(f32[128,1024]{1,0:T(8,128)S(1)} %get-tuple-element.18.refs_0_, bf16[128,1024]{1,0:T(8,128)(2,1)S(1)} %get-tuple-element.19.refs_1_, ...), custom_call_target="tpu_custom_call" | custom-call | tf_op jit(solution)/shard_map/pallas_call | solution.py:502

commit v3 on v2

--- a/solution.py
+++ b/solution.py
@@ -1,4 +1,5 @@
 import functools
+import itertools
 
 import jax
 import jax.numpy as jnp
@@ -10,8 +11,10 @@
 MESH = pl.DeviceIdType.MESH
 F32 = jnp.float32
 BF16 = jnp.bfloat16
-SKEW = 2
+SKEW = 3
 GROUP = 4
+PAIR = 2
+REST = 4
 
 
 def split(x):
@@ -262,23 +265,31 @@
         key2 = split(key)
         beta_row, beta_col = beta_of(h)
         reads = mm(split(jnp.concatenate([w_rows, reader], axis=0)), state2)
+        yield
         corrected = u_rows - reads[:count]
         mixed_ref[:, lanes] = reads[count:] + mm(split(score), split(u_rows))
         d_corr = mm(split(score.T), (cot, None)) + mm(key2, adj2)
+        yield
         corr2 = split(corrected)
         d_score = jnp.where(lower, mm((cot, None), corr2, True), 0.0)
+        yield
         back = mm(split(jnp.concatenate([cot.astype(F32), d_corr], axis=0)), state2, True)
+        yield
         y = mm(split(inv_s[h].T), split(jnp.concatenate([-back[count:], d_corr], axis=1)))
         y_k, y_v = y[:, :width], y[:, width:]
+        yield
         d_low = jnp.where(strict, -mm(split(y), split(wu), True), 0.0)
+        yield
         d_beta = jnp.sum(y_k * key + y_v * value + d_low * gram_s[h], axis=1, keepdims=True)
         d_gram = beta_col * d_low
         onto = mm(split(jnp.concatenate([d_score, d_gram + d_gram.T], axis=0)), key2)
+        yield
         d_query = back[:count] + onto[:count]
         d_key = (
             mm(split(d_score.T), split(query)) + mm(corr2, adj2, True)
             + beta_col * y_k + onto[count:]
         )
+        yield
         d_value = beta_col * y_v
         d_row = jnp.sum(jnp.where(eye, d_beta, 0.0), axis=0, keepdims=True)
         dbeta_ref[pl.ds(h, 1), :] = d_row * beta_row * (1.0 - beta_row)
@@ -289,6 +300,7 @@
                 grad = grad - unit * jnp.sum(grad * unit, axis=1, keepdims=True)
             d_pre = grad * g_s[s, h]
             ext = jnp.concatenate([blank, d_pre, blank], axis=0)
+            yield
             series = series_of(s, h)
             full = None
             for j in range(4):
@@ -302,12 +314,9 @@
             grads[s][:, lanes] = full[8:].astype(BF16)
             tail[h, s * 8:s * 8 + 8, :] = full[count:]
 
-        @pl.when(z > 0)
-        def _():
-            edge_copy(h).start()
-
     early = z < shards // 2
     lag_state = jnp.where(early, 0, SKEW)
+    lag_end = jnp.where(first | last, SKEW, SKEW + REST)
     lag_adj = jnp.where(early, SKEW, 0)
 
     def chain(step, carry):
@@ -332,9 +341,18 @@
                 out_adj[ha] = out_adj[ha] + advance(nt_s[ha], in_adj[ha])
                 adj_copy(ha).start()
 
-        @pl.when(step >= SKEW)
+        done = step - lag_end
+
+        @pl.when((done >= 0) & (done < heads) & (lax.rem(done, PAIR) == PAIR - 1))
         def _():
-            finish(step - SKEW)
+            ids = [done - PAIR + 1 + i for i in range(PAIR)]
+            for _ in itertools.zip_longest(*[finish(h) for h in ids]):
+                pass
+
+            @pl.when(z > 0)
+            def _():
+                for h in ids:
+                    edge_copy(h).start()
 
         if scatter:
             @pl.when(step == SKEW)
@@ -346,7 +364,7 @@
 
         return carry
 
-    lax.fori_loop(0, heads + SKEW, chain, 0)
+    lax.fori_loop(0, heads + SKEW + REST, chain, 0)
 
     if scatter:
         if parts > 1:

time: 44.1 us -> 41.3 us (0.937)
  Pallas kernels: 43.3 us -> 40.5 us
    pallas_call x1, Pallas kernels: 42.2 us -> 39.4 us  [per_device(): pl.pallas_call(functools.partial(kernel, shards, parts, scatter), out_sha...]
where the time goes in v3:
time: 41.3 us; the launch traced here: 41.2 us
  Pallas kernels  40.5 us (98%)
  between operations  0.64 us (2%)
    pallas_call x1, Pallas kernels, per_device(): pl.pallas_call(functools.partial(kernel, shards, parts, scatter), out_sha...  39.4 us
    pallas_call x1, Pallas kernels, per_device(): pl.pallas_call(functools.partial(flush, 5), out_shape=(*(jax.ShapeDtypeSt...  1.11 us

profile of v3, /device:TPU:0, one launch (start us, length us, event | category | flops | bytes accessed | tf_op | source)
XLA Modules:
  0.0 41.2 jit_solution(2513591363288318357)
XLA Ops:
  0.6 39.4 %shard_map.109 = (f32[128,1024]{1,0:T(8,128)S(1)}, bf16[128,1024]{1,0:T(8,128)(2,1)S(1)}, bf16[128,1024]{1,0:T(8,128)(2,1)S(1)}, bf16[128,1024]{1,0:T(8,128)(2,1...) custom-call(bf16[128,1024]{1,0:T(8,128)(2,1)} %bitcast.11, bf16[128,1024]{1,0:T(8,128)(2,1)} %bitcast.12, ...), custom_call_target="tpu_custom_call" | custom-call | tf_op jit(solution)/shard_map/pallas_call | solution.py:468
  40.1 1.1 %shard_map.110 = (f32[128,1024]{1,0:T(8,128)}, bf16[128,1024]{1,0:T(8,128)(2,1)}, bf16[128,1024]{1,0:T(8,128)(2,1)}, bf16[128,1024]{1,0:T(8,128)(2,1)}, f32[8,128]{1,0:T(8,128)}, /*index=5*/f32[96,16]{1,0:T(8,128)}) custom-call(f32[128,1024]{1,0:T(8,128)S(1)} %get-tuple-element.18.refs_0_, bf16[128,1024]{1,0:T(8,128)(2,1)S(1)} %get-tuple-element.19.refs_1_, ...), custom_call_target="tpu_custom_call" | custom-call | tf_op jit(solution)/shard_map/pallas_call | solution.py:520
